TPU v7x, 256 devices: a whole 4x4x8 slice. The times are simulated.
256 devices in a mesh: seq: 8 (over y, core), vocab: 32 (over z, x).
Axes of the slice: x: 4, y: 4, z: 8, core: 2. Of those that a mesh axis runs over, the one named last changes fastest.
Arguments:
- hidden: bfloat16 [2, 1024, 5120], P(None, 'seq'), may hold values from -128 to 128
- head_weight: bfloat16 [5120, 77824], P('seq', 'vocab'), may hold values from -1 to 1
- ref_logits: bfloat16 [2, 1024, 77824], P(None, 'seq', 'vocab'), may hold values from -320 to 320
- token_ids: int32 [2, 1024], P(None, 'seq'), may hold values from 0 to 77823
- end_pos: int32 [2], replicated, may hold values from 512 to 1023
- loss_mask: int32 [2, 1024], P(None, 'seq'), may hold values 0 or 1
- scores: float32 [2], replicated, may hold values from -8 to 8
Outputs:
- logit_grad: bfloat16 [2, 1024, 77824], P(None, 'seq', 'vocab')
- hidden_grad: bfloat16 [2, 1024, 5120], P(None, 'seq', 'vocab')
- advantages: float32 [2, 1024], P(None, 'seq')
All inputs are finite; a program needn't handle non-finite values. No bound on the sum of `loss_mask` on one device may be relied on, other than what follows from the above.
Results may differ from a plain program's by a relative error of at most 0.0039.
The roundings to bfloat16 on the way count: a program that leaves them out, or rounds other values in their place, can miss the bound.
Values may be sent and summed in bfloat16 or wider, within the bound.
No kernel may reach another device: no remote copies, remote signals or barrier semaphores. Data moves between devices by JAX's collectives and lax.ppermute only.
A program may use at most 128 MiB of HBM per device.

v0:
```python
import jax
import jax.numpy as jnp
from jax import lax
from jax.sharding import Mesh, PartitionSpec as P

SEQ = ("y", "c")
VOC = ("z", "x")
BOUNDS = ((0, 256), (256, 512), (512, 640))


def spread(value, axes):
    count = lax.axis_size(axes)
    return lax.all_to_all(jnp.broadcast_to(value[None], (count,) + value.shape), axes, 0, 0)


def per_device(hidden, head_weight, ref_logits, token_ids, end_pos, loss_mask, scores):
    batch, segment, width = hidden.shape
    rows = batch * segment
    depth, vocab_dev = head_weight.shape
    seqs = lax.axis_size(SEQ)
    seq_index = lax.axis_index(SEQ)
    seq_start = seq_index * segment
    vocab_start = lax.axis_index(VOC) * vocab_dev
    heads = [lax.all_gather(head_weight[lo:hi], SEQ, axis=0, tiled=True) for lo, hi in BOUNDS]
    refs = ref_logits.astype(jnp.float32).reshape(rows, vocab_dev)
    ref_top = jnp.max(refs, axis=1)
    ref_lse = ref_top + jnp.log(jnp.sum(jnp.exp(refs - ref_top[:, None]), axis=1))
    states = hidden.reshape(rows, seqs, depth)
    logits = None
    for (lo, hi), head in zip(BOUNDS, heads):
        term = jnp.dot(
            states[:, :, lo:hi].reshape(rows, seqs * (hi - lo)),
            head,
            preferred_element_type=jnp.float32,
        )
        logits = term if logits is None else logits + term
    top = jnp.max(logits, axis=1)
    expo = jnp.exp(logits - top[:, None])
    stats = jnp.stack(
        [top, jnp.sum(expo, axis=1), jnp.sum(expo * (logits - refs), axis=1), ref_lse]
    )
    stats = spread(stats, VOC)
    tops = stats[:, 0]
    top_policy = jnp.max(tops, axis=0)
    scale = jnp.exp(tops - top_policy[None])
    total = jnp.sum(stats[:, 1] * scale, axis=0)
    weighted = jnp.sum(stats[:, 2] * scale, axis=0)
    top_ref = jnp.max(stats[:, 3], axis=0)
    lse_ref = top_ref + jnp.log(jnp.sum(jnp.exp(stats[:, 3] - top_ref[None]), axis=0))
    lse_policy = top_policy + jnp.log(total)
    kl_value = (weighted / total - lse_policy + lse_ref).reshape(batch, segment)
    position = seq_start + lax.broadcasted_iota(jnp.int32, (1, segment), 1)
    live = ((loss_mask == 1) & (position <= end_pos[:, None])).astype(jnp.float32)
    at_end = (position == end_pos[:, None]).astype(jnp.float32)
    reward = -0.01 * kl_value * live + scores[:, None] * at_end
    both = spread(jnp.stack([reward, live]), SEQ)
    rewards, lives = (both[:, 0], both[:, 1])
    upper = (
        lax.broadcasted_iota(jnp.int32, (segment, segment), 0)
        >= lax.broadcasted_iota(jnp.int32, (segment, segment), 1)
    ).astype(jnp.float32)
    suffix = jnp.dot(
        rewards.reshape(seqs * batch, segment), upper, precision=lax.Precision.HIGHEST
    ).reshape(seqs, batch, segment)
    totals = jnp.sum(rewards, axis=2)
    later = (
        lax.broadcasted_iota(jnp.int32, (seqs, seqs, 1), 1)
        > lax.broadcasted_iota(jnp.int32, (seqs, seqs, 1), 0)
    ).astype(jnp.float32)
    carried = jnp.sum(later * totals[None], axis=1)
    returns_all = suffix + carried[:, :, None]
    count = jnp.maximum(jnp.sum(lives), 1.0)
    mean = jnp.sum(lives * returns_all) / count
    var = jnp.sum(lives * returns_all * returns_all) / count - mean * mean
    returns = lax.dynamic_index_in_dim(returns_all, seq_index, 0, keepdims=False)
    advantages = (returns - mean) / jnp.sqrt(var + 1e-05)
    factor = live * advantages / count
    prob = jnp.exp(logits - lse_policy[:, None])
    column = vocab_start + lax.broadcasted_iota(jnp.int32, (1, vocab_dev), 1)
    onehot = (column == token_ids.reshape(rows, 1)).astype(jnp.float32)
    logit_grad = (factor.reshape(rows, 1) * (prob - onehot)).astype(jnp.bfloat16)
    pieces = []
    for (lo, hi), head in zip(BOUNDS[::-1], heads[::-1]):
        part = lax.dot_general(
            head, logit_grad, (((1,), (1,)), ((), ())), preferred_element_type=jnp.float32
        ).reshape(seqs, hi - lo, rows)
        pieces.append(lax.psum_scatter(part, "z", scatter_dimension=0, tiled=False))
    mine = jnp.concatenate(pieces[::-1], axis=0)
    mine = mine.reshape(lax.axis_size("x"), depth // lax.axis_size("x"), rows)
    mine = lax.psum_scatter(mine, "x", scatter_dimension=0, tiled=False)
    hidden_grad = mine.T.reshape(batch, segment, -1).astype(jnp.bfloat16)
    return (logit_grad.reshape(batch, segment, vocab_dev), hidden_grad, advantages)


def solution(mesh):
    chips = mesh.devices.reshape(4, 2, 8, 4)
    fine = Mesh(chips, ("y", "c", "z", "x"))
    in_specs = (
        P(None, SEQ, None),
        P(SEQ, VOC),
        P(None, SEQ, VOC),
        P(None, SEQ),
        P(),
        P(None, SEQ),
        P(),
    )
    out_specs = (P(None, SEQ, VOC), P(None, SEQ, VOC), P(None, SEQ))
    return jax.shard_map(
        per_device, mesh=fine, in_specs=in_specs, out_specs=out_specs, check_vma=False
    )
```

profile of v0, /device:TPU:8, one launch (start us, length us, event | category | flops | bytes accessed | tf_op | source)
XLA Modules:
  0.0 374.6 jit_solution(1781459673582744261)
XLA Ops:
  7.2 0.0 all-gather.4.cloned.1.call-start
  7.2 3.4 fusion.19
  10.6 0.0 all-gather.6.cloned.1.call-start
  10.7 0.7 all-gather.6.cloned.1.call-update
  11.4 0.0 all-gather.8.cloned.1.call-start
  11.4 2.0 slice.42
  13.4 0.5 copy.58
  13.9 0.1 fusion.20
  14.1 1.3 copy.59
  15.4 1.3 copy.60
  16.7 0.2 reduce_max.42
  16.9 0.6 exponential_reduce_fusion
  17.5 54.3 %all-gather.4.cloned.1.call-done = bf16[2048,2432]{1,0:T(8,128)(2,1)} async-done(((bf16[256,2432]{1,0:T(8,128)(2,1)}), bf16[2048,2432]{1,0:T(8,128)(2,1)}) %all-gather.4.cloned.1.call-update) | async-done | bytes 9961488 | tf_op jit(solution)/shard_map/all_gather | solution.py:24
  71.8 8.3 %fusion.22 = f32[256,2432]{1,0:T(8,128)} fusion(bf16[256,2048]{1,0:T(8,128)(2,1)S(1)} %bitcast.124, bf16[2048,2432]{1,0:T(8,128)(2,1)} %all-gather.4.cloned.1.call-done), kind=kOutput, calls=%fused_computation.60 | convolution fusion | flops 2550136832 | bytes 13500416 | tf_op jit(solution)/shard_map/dot_general | solution.py:31
  80.1 53.3 %all-gather.6.cloned.1.call-done = bf16[2048,2432]{1,0:T(8,128)(2,1)} async-done(((bf16[256,2432]{1,0:T(8,128)(2,1)}), bf16[2048,2432]{1,0:T(8,128)(2,1)}) %all-gather.6.cloned.1.call-update) | async-done | bytes 9961488 | tf_op jit(solution)/shard_map/all_gather | solution.py:24
  133.4 8.3 %convolution_add_fusion.1 = f32[256,2432]{1,0:T(8,128)} fusion(f32[256,2432]{1,0:T(8,128)} %fusion.22, bf16[256,2048]{1,0:T(8,128)(2,1)S(1)} %bitcast.123, bf16[2048,2432]{1,0:T(8,128)(2,1)} %all-gather.6.cloned.1.call-done), kind=kOutput, calls=%fused_computation.1 | convolution fusion | flops 2550759424 | bytes 15990784 | tf_op jit(solution)/shard_map/dot_general | solution.py:31
  141.8 31.5 %all-gather.8.cloned.1.call-done = bf16[1024,2432]{1,0:T(8,128)(2,1)} async-done(((bf16[128,2432]{1,0:T(8,128)(2,1)}), bf16[1024,2432]{1,0:T(8,128)(2,1)}) %all-gather.8.cloned.1.call-update) | async-done | bytes 4980752 | tf_op jit(solution)/shard_map/all_gather | solution.py:24
  173.3 4.9 %fusion.21 = (f32[256]{0:T(256)S(1)}, f32[256,2432]{1,0:T(8,128)S(1)}) fusion(f32[256,2432]{1,0:T(8,128)} %convolution_add_fusion.1, bf16[1024,2432]{1,0:T(8,128)(2,1)} %all-gather.8.cloned.1.call-done, bf16[32,8,8,128]{3,2,1,0:T(8,128)(2,1)S(1)} %bitcast.119), kind=kOutput, calls=%fused_computation.59 | convolution fusion | flops 1276313344 | bytes 10486784 | tf_op jit(solution)/shard_map/dot_general | solution.py:31
  178.2 0.9 fusion.2
  179.1 0.7 broadcast_in_dim.4
  179.8 9.8 %all-to-all-start = ((f32[32,4,256]{2,1,0:T(4,128)}), f32[32,4,256]{2,1,0:T(4,128)S(1)}, u32[]{:S(2)}, u32[]{:S(2)}) async-start(f32[32,4,256]{2,1,0:T(4,128)} %broadcast_in_dim.4), calls=%async_computation | async-start | bytes 262144 | tf_op jit(solution)/shard_map/all_to_all | solution.py:13
  189.7 10.8 %all-to-all-done = f32[32,4,256]{2,1,0:T(4,128)S(1)} async-done(((f32[32,4,256]{2,1,0:T(4,128)}), f32[32,4,256]{2,1,0:T(4,128)S(1)}, u32[]{:S(2)}, u32[]{:S(2)}) %all-to-all-start) | async-done | bytes 131104 | tf_op jit(solution)/shard_map/all_to_all | solution.py:13
  200.5 0.1 slice_reduce_fusion.2
  200.7 0.1 fusion.18
  200.8 0.6 broadcast_in_dim.5
  201.4 4.8 %all-to-all-start.1 = ((f32[8,2,2,128]{3,2,1,0:T(2,128)}), f32[8,2,2,128]{3,2,1,0:T(2,128)S(1)}, u32[]{:S(2)}, u32[]{:S(2)}) async-start(f32[8,2,2,128]{3,2,1,0:T(2,128)} %broadcast_in_dim.5), calls=%async_computation.1 | async-start | bytes 32768 | tf_op jit(solution)/shard_map/all_to_all | solution.py:13
  206.2 3.9 %all-to-all-done.1 = f32[8,2,2,128]{3,2,1,0:T(2,128)S(1)} async-done(((f32[8,2,2,128]{3,2,1,0:T(2,128)}), f32[8,2,2,128]{3,2,1,0:T(2,128)S(1)}, u32[]{:S(2)}, u32[]{:S(2)}) %all-to-all-start.1) | async-done | bytes 16416 | tf_op jit(solution)/shard_map/all_to_all | solution.py:13
  210.1 0.6 slice_reduce_fusion
  210.7 0.1 copy.55
  210.8 0.1 multiply_reduce_fusion.1
  211.5 0.8 fusion.15
  213.7 0.8 multiply_convert_fusion
  214.6 1.0 copy-done.3
  215.6 4.0 %convolution_bitcast_fusion.2 = f32[1024,256]{0,1:T(8,128)S(1)} fusion(bf16[256,2432]{1,0:T(8,128)(2,1)S(1)} %multiply_convert_fusion, bf16[1024,2432]{1,0:T(8,128)(2,1)} %all-gather.8.cloned.1.call-done), kind=kOutput, calls=%fused_computation.11 | convolution fusion | flops 1275068416 | bytes 7274496 | tf_op jit(solution)/shard_map/dot_general | solution.py:84
  219.6 1.3 copy.46
  220.9 0.2 reduce-scatter.5.cloned.1.call-start
  221.2 5.5 %convolution_bitcast_fusion.1 = f32[2048,256]{0,1:T(8,128)S(1)} fusion(bf16[256,2432]{1,0:T(8,128)(2,1)S(1)} %copy-done.4, bf16[2048,2432]{1,0:T(8,128)(2,1)} %all-gather.4.cloned.1.call-done), kind=kOutput, calls=%fused_computation.3 | convolution fusion | flops 2550136832 | bytes 13303808 | tf_op jit(solution)/shard_map/dot_general | solution.py:84
  226.7 1.8 copy.44
  228.6 0.0 reduce-scatter.7.cloned.1.call-start
  228.6 5.5 %convolution_bitcast_fusion = f32[2048,256]{0,1:T(8,128)S(1)} fusion(bf16[256,2432]{1,0:T(8,128)(2,1)S(1)} %copy-done.4, bf16[2048,2432]{1,0:T(8,128)(2,1)} %all-gather.6.cloned.1.call-done), kind=kOutput, calls=%fused_computation.2 | convolution fusion | flops 2550136832 | bytes 13303808 | tf_op jit(solution)/shard_map/dot_general | solution.py:84
  234.2 1.9 copy.45
  236.1 0.0 reduce-scatter.11.cloned.1.call-start
  236.1 17.7 %reduce-scatter.9.cloned.1.call-done = f32[1,128,256]{2,1,0:T(8,128)} async-done(((f32[8,128,256]{2,1,0:T(8,128)}), f32[1,128,256]{2,1,0:T(8,128)}) %reduce-scatter.9.cloned.1.call-update) | async-done | bytes 131088 | tf_op jit(solution)/shard_map/reduce_scatter | solution.py:87
  253.8 43.1 %reduce-scatter.5.cloned.1.call-done = f32[1,256,256]{2,1,0:T(8,128)} async-done(((f32[8,256,256]{2,1,0:T(8,128)}), f32[1,256,256]{2,1,0:T(8,128)}) %reduce-scatter.5.cloned.1.call-update) | async-done | bytes 262160 | tf_op jit(solution)/shard_map/reduce_scatter | solution.py:87
  296.9 43.7 %reduce-scatter.7.cloned.1.call-done = f32[1,256,256]{2,1,0:T(8,128)} async-done(((f32[8,256,256]{2,1,0:T(8,128)}), f32[1,256,256]{2,1,0:T(8,128)}) %reduce-scatter.7.cloned.1.call-update) | async-done | bytes 262160 | tf_op jit(solution)/shard_map/reduce_scatter | solution.py:87
  340.6 2.0 pad_maximum_fusion
  342.6 23.7 %reduce-scatter.11.cloned.1.call-done = f32[1,160,256]{2,1,0:T(8,128)} async-done(((f32[4,160,256]{2,1,0:T(8,128)}), f32[1,160,256]{2,1,0:T(8,128)}) %reduce-scatter.11.cloned.1.call-update) | async-done | bytes 163856 | tf_op jit(solution)/shard_map/reduce_scatter | solution.py:90
  366.2 1.6 copy_bitcast_fusion
  (42 shorter events, 0.3 us)
Async XLA Ops:
  7.2 64.6 %all-gather.4.cloned.1.call-start = ((), (), s32[]{:S(2)}) async-start(), calls=%async_computation.6 | async-start | bytes 11206656 | tf_op jit(solution)/shard_map/all_gather | solution.py:24
  10.6 2.8 copy-start.2
  10.6 122.8 %all-gather.6.cloned.1.call-start = ((), (), s32[]{:S(2)}) async-start(), calls=%async_computation.7 | async-start | bytes 11206656 | tf_op jit(solution)/shard_map/all_gather | solution.py:24
  11.4 161.9 %all-gather.8.cloned.1.call-start = ((), (), s32[]{:S(2)}) async-start(), calls=%async_computation.8 | async-start | bytes 5603328 | tf_op jit(solution)/shard_map/all_gather | solution.py:24
  14.1 2.6 copy-start
  16.7 55.2 %copy-start.6 = (bf16[32,8,8,256]{3,1,2,0:T(8,128)(2,1)S(1)}, bf16[32,8,8,256]{3,1,2,0:T(8,128)(2,1)}, u32[]{:S(2)}) copy-start(bf16[32,8,8,256]{3,1,2,0:T(8,128)(2,1)} %copy.59) | copy-start | bytes 3145732
  71.8 61.6 %copy-start.5 = (bf16[32,8,8,256]{3,1,2,0:T(8,128)(2,1)S(1)}, bf16[32,8,8,256]{3,1,2,0:T(8,128)(2,1)}, u32[]{:S(2)}) copy-start(bf16[32,8,8,256]{3,1,2,0:T(8,128)(2,1)} %copy.60) | copy-start | bytes 3145732
  173.3 5.0 %copy-start.1 = (bf16[2,128,2432]{2,1,0:T(8,128)(2,1)S(1)}, bf16[2,128,2432]{2,1,0:T(8,128)(2,1)}, u32[]{:S(2)}) copy-start(bf16[2,128,2432]{2,1,0:T(8,128)(2,1)} %param.9) | copy-start | bytes 3735556
  178.2 22.5 %copy-start.9 = (s32[2,128]{1,0:T(2,128)S(1)}, s32[2,128]{1,0:T(2,128)}, u32[]{:S(2)}) copy-start(s32[2,128]{1,0:T(2,128)} %param.12) | copy-start | bytes 3076
  178.2 22.5 %copy-start.10 = (f32[2]{0:T(128)S(1)}, f32[2]{0:T(128)}, u32[]{:S(2)}) copy-start(f32[2]{0:T(128)} %param.13) | copy-start | bytes 28
  178.2 22.5 %copy-start.11 = (s32[2]{0:T(128)S(1)}, s32[2]{0:T(128)}, u32[]{:S(2)}) copy-start(s32[2]{0:T(128)} %param.11) | copy-start | bytes 28
  178.2 35.5 %copy-start.8 = (s32[2,128]{1,0:T(2,128)S(1)}, s32[2,128]{1,0:T(2,128)}, u32[]{:S(2)}) copy-start(s32[2,128]{1,0:T(2,128)} %param.10) | copy-start | bytes 3076
  179.8 20.7 %all-to-all-start = ((f32[32,4,256]{2,1,0:T(4,128)}), f32[32,4,256]{2,1,0:T(4,128)S(1)}, u32[]{:S(2)}, u32[]{:S(2)}) async-start(f32[32,4,256]{2,1,0:T(4,128)} %broadcast_in_dim.4), calls=%async_computation | async-start | bytes 262144 | tf_op jit(solution)/shard_map/all_to_all | solution.py:13
  201.4 8.7 %all-to-all-start.1 = ((f32[8,2,2,128]{3,2,1,0:T(2,128)}), f32[8,2,2,128]{3,2,1,0:T(2,128)S(1)}, u32[]{:S(2)}, u32[]{:S(2)}) async-start(f32[8,2,2,128]{3,2,1,0:T(2,128)} %broadcast_in_dim.5), calls=%async_computation.1 | async-start | bytes 32768 | tf_op jit(solution)/shard_map/all_to_all | solution.py:13
  206.2 47.6 %reduce-scatter.9.cloned.1.call-start = ((), (), s32[]{:S(2)}) async-start(), calls=%async_computation.11 | async-start | bytes 1179648 | tf_op jit(solution)/shard_map/reduce_scatter | solution.py:87
  213.7 5.9 %copy-start.7 = (f32[1,2,128]{2,0,1:T(1,128)}, f32[1,2,128]{2,0,1:T(1,128)S(1)}, u32[]{:S(2)}) copy-start(f32[1,2,128]{2,0,1:T(1,128)S(1)} %subtract_divide_fusion) | copy-start | bytes 3076
  214.6 1.0 copy-start.3
  219.6 1.6 copy-start.4
  220.9 75.9 %reduce-scatter.5.cloned.1.call-start = ((), (), s32[]{:S(2)}) async-start(), calls=%async_computation.9 | async-start | bytes 2359296 | tf_op jit(solution)/shard_map/reduce_scatter | solution.py:87
  228.6 112.0 %reduce-scatter.7.cloned.1.call-start = ((), (), s32[]{:S(2)}) async-start(), calls=%async_computation.10 | async-start | bytes 2359296 | tf_op jit(solution)/shard_map/reduce_scatter | solution.py:87
  236.1 130.2 %reduce-scatter.11.cloned.1.call-start = ((), (), s32[]{:S(2)}) async-start(), calls=%async_computation.12 | async-start | bytes 819200 | tf_op jit(solution)/shard_map/reduce_scatter | solution.py:90
Sparse Core Ops, SparseCore 0:
  10.7 61.0 all-gather.3
  74.2 59.1 all-gather.5
  135.2 37.9 all-gather.7
  221.0 32.6 reduce-scatter.8
  256.2 40.6 reduce-scatter.4
  299.3 41.2 reduce-scatter.6
  343.1 23.0 reduce-scatter.10
where the time goes:
time: 375 us
  waiting for transfers between devices  283 us (75%)
  matrix products  37.4 us (10%)
  between operations  16.4 us (4%)
  local copies, waits for them, and re-layouts  16 us (4%)
  starting transfers between devices  15 us (4%)
  other arithmetic  7.08 us (2%)
    all_gather x3, waiting for transfers between devices, per_device(): lax.all_gather(head_weight[lo:hi], SEQ, axis=0, tiled=True)  139 us
    reduce_scatter x3, waiting for transfers between devices, per_device(): pieces.append(lax.psum_scatter(part, 'z', scatter_dimension=0, tiled=False))  104 us
    reduce_scatter x1, waiting for transfers between devices, per_device(): mine = lax.psum_scatter(mine, 'x', scatter_dimension=0, tiled=False)  23.7 us
    dot_general x3, matrix products, per_device(): jnp.dot(states[:, :, lo:hi].reshape(rows, seqs * (hi - lo)), head, prefer...  21.5 us
    dot_general x3, matrix products, per_device(): lax.dot_general(head, logit_grad, (((1,), (1,)), ((), ())), preferred_ele...  15 us
    all_to_all x2, waiting for transfers between devices, spread(): lax.all_to_all(jnp.broadcast_to(value[None], (count,) + value.shape), axe...  14.7 us
    all_to_all x2, starting transfers between devices, spread(): lax.all_to_all(jnp.broadcast_to(value[None], (count,) + value.shape), axe...  14.6 us
  transfers between devices with their start and end apart: 9, of which 9 were waited for; matrix products, arithmetic and copies ran while one was open for 10% of the time, Pallas kernels for 0%

commit v1 on v0

--- a/solution.py
+++ b/solution.py
@@ -2,6 +2,7 @@
 import jax.numpy as jnp
 from jax import lax
 from jax.sharding import Mesh, PartitionSpec as P
+from jax.lax import all_to_all, psum
 
 SEQ = ("y", "c")
 VOC = ("z", "x")
@@ -21,7 +22,15 @@
     seq_index = lax.axis_index(SEQ)
     seq_start = seq_index * segment
     vocab_start = lax.axis_index(VOC) * vocab_dev
-    heads = [lax.all_gather(head_weight[lo:hi], SEQ, axis=0, tiled=True) for lo, hi in BOUNDS]
+
+    def open_weights_for(local_array):
+        moved = jnp.concatenate(
+            all_to_all(jnp.stack([local_array for _ in range(psum(1, SEQ))], axis=0), SEQ, 0, 0),
+            axis=0,
+        )
+        return moved
+
+    heads = [open_weights_for(head_weight[lo:hi]) for lo, hi in BOUNDS]
     refs = ref_logits.astype(jnp.float32).reshape(rows, vocab_dev)
     ref_top = jnp.max(refs, axis=1)
     ref_lse = ref_top + jnp.log(jnp.sum(jnp.exp(refs - ref_top[:, None]), axis=1))

time: 375 us -> 520 us (1.39)
  blocking collectives: 0 us -> 117 us
  starting transfers between devices: 15 us -> 27.6 us
  local copies, waits for them, and re-layouts: 16 us -> 25.6 us
    all_to_all x0 -> x2, waiting for transfers between devices: none -> 144 us  [open_weights_for(): all_to_all(jnp.stack([local_array for _ in range(psum(1, SEQ))], axis=0),...]
    all_gather x3 -> x0, waiting for transfers between devices: 139 us -> none  [per_device(): lax.all_gather(head_weight[lo:hi], SEQ, axis=0, tiled=True)]
    all_to_all x0 -> x1, blocking collectives: none -> 117 us  [open_weights_for(): all_to_all(jnp.stack([local_array for _ in range(psum(1, SEQ))], axis=0),...]
    all_to_all x0 -> x2, starting transfers between devices: none -> 13.2 us  [open_weights_for(): all_to_all(jnp.stack([local_array for _ in range(psum(1, SEQ))], axis=0),...]
    another operation x0 -> x3, local copies, waits for them, and re-layouts: none -> 9.02 us  [open_weights_for(): jnp.stack([local_array for _ in range(psum(1, SEQ))], axis=0)]
  transfers between devices with their start and end apart: 9 -> 8, of which waited for: 9 -> 8; matrix products, arithmetic and copies ran while one was open for 10% -> 7% of each run, Pallas kernels for 0% -> 0%
where the time goes in v1:
time: 520 us; the launch traced here: 519 us
  waiting for transfers between devices  287 us (55%)
  blocking collectives  117 us (22%)
  matrix products  38 us (7%)
  starting transfers between devices  27.6 us (5%)
  local copies, waits for them, and re-layouts  25.6 us (5%)
  between operations  16 us (3%)
  other arithmetic  8.74 us (2%)
    all_to_all x2, waiting for transfers between devices, open_weights_for(): all_to_all(jnp.stack([local_array for _ in range(psum(1, SEQ))], axis=0),...  144 us
    all_to_all x1, blocking collectives, open_weights_for(): all_to_all(jnp.stack([local_array for _ in range(psum(1, SEQ))], axis=0),...  117 us
    reduce_scatter x3, waiting for transfers between devices, per_device(): pieces.append(lax.psum_scatter(part, 'z', scatter_dimension=0, tiled=False))  105 us
    reduce_scatter x1, waiting for transfers between devices, per_device(): mine = lax.psum_scatter(mine, 'x', scatter_dimension=0, tiled=False)  23.7 us
    dot_general x3, matrix products, per_device(): jnp.dot(states[:, :, lo:hi].reshape(rows, seqs * (hi - lo)), head, prefer...  21.8 us
    dot_general x3, matrix products, per_device(): lax.dot_general(head, logit_grad, (((1,), (1,)), ((), ())), preferred_ele...  15.5 us
    all_to_all x2, waiting for transfers between devices, spread(): lax.all_to_all(jnp.broadcast_to(value[None], (count,) + value.shape), axe...  14.4 us
    all_to_all x2, starting transfers between devices, spread(): lax.all_to_all(jnp.broadcast_to(value[None], (count,) + value.shape), axe...  14.3 us
  transfers between devices with their start and end apart: 8, of which 8 were waited for; matrix products, arithmetic and copies ran while one was open for 7% of the time, Pallas kernels for 0%

profile of v1, /device:TPU:8, one launch (start us, length us, event | category | flops | bytes accessed | tf_op | source)
XLA Modules:
  0.0 519.4 jit_solution(12993867322957408198)
XLA Ops:
  7.2 1.1 slice.42
  8.3 2.6 stack.25
  10.9 6.7 %all-to-all-start.2 = ((bf16[8,128,2432]{2,1,0:T(8,128)(2,1)}), bf16[8,128,2432]{2,1,0:T(8,128)(2,1)}, u32[]{:S(2)}, u32[]{:S(2)}) async-start(bf16[8,128,2432]{2,1,0:T(8,128)(2,1)} %stack.25), calls=%async_computation.2 | async-start | bytes 9961472 | tf_op jit(solution)/shard_map/all_to_all | solution.py:28
  17.6 2.9 fusion.22
  20.5 53.9 %all-to-all-done.2 = bf16[8,128,2432]{2,1,0:T(8,128)(2,1)} async-done(((bf16[8,128,2432]{2,1,0:T(8,128)(2,1)}), bf16[8,128,2432]{2,1,0:T(8,128)(2,1)}, u32[]{:S(2)}, u32[]{:S(2)}) %all-to-all-start.2) | async-done | bytes 4980768 | tf_op jit(solution)/shard_map/all_to_all | solution.py:28
  74.4 2.0 stack.24
  76.4 116.5 %all_to_all.25 = bf16[8,256,2432]{2,1,0:T(8,128)(2,1)} all-to-all(bf16[8,256,2432]{2,1,0:T(8,128)(2,1)S(1)} %stack.24), channel_id=1, replica_groups=mesh['y'=4,'c'=2,'z'=8,'x'=4] {'y','c'}, dimensions={0} | all-to-all | bytes 19922944 | tf_op jit(solution)/shard_map/all_to_all | solution.py:28
  192.9 4.4 stack.23
  197.4 6.4 %all-to-all-start = ((bf16[8,256,2432]{2,1,0:T(8,128)(2,1)}), bf16[8,256,2432]{2,1,0:T(8,128)(2,1)}, u32[]{:S(2)}, u32[]{:S(2)}) async-start(bf16[8,256,2432]{2,1,0:T(8,128)(2,1)} %stack.23), calls=%async_computation | async-start | bytes 19922944 | tf_op jit(solution)/shard_map/all_to_all | solution.py:28
  203.8 2.3 copy.73
  206.1 1.5 copy-done.1
  207.7 0.3 reduce_max.42
  208.0 0.6 exponential_reduce_fusion
  208.5 1.7 fusion.23
  210.2 5.4 %convolution_bitcast_fusion = f32[256,2432]{1,0:T(8,128)} fusion(bf16[8,128,2432]{2,1,0:T(8,128)(2,1)} %all-to-all-done.2, bf16[256,8,128]{2,1,0:T(8,128)(2,1)S(1)} %slice.51), kind=kOutput, calls=%fused_computation | convolution fusion | flops 1275068416 | bytes 7995392 | tf_op jit(solution)/shard_map/dot_general | solution.py:40
  215.7 8.1 %convolution_bitcast_fusion.1 = f32[256,2432]{1,0:T(8,128)} fusion(bf16[8,256,2432]{2,1,0:T(8,128)(2,1)} %all_to_all.25, bf16[256,8,256]{2,1,0:T(8,128)(2,1)S(1)} %get-tuple-element.31), kind=kOutput, calls=%fused_computation.1 | convolution fusion | flops 2550136832 | bytes 13500416 | tf_op jit(solution)/shard_map/dot_general | solution.py:40
  223.8 90.2 %all-to-all-done = bf16[8,256,2432]{2,1,0:T(8,128)(2,1)} async-done(((bf16[8,256,2432]{2,1,0:T(8,128)(2,1)}), bf16[8,256,2432]{2,1,0:T(8,128)(2,1)}, u32[]{:S(2)}, u32[]{:S(2)}) %all-to-all-start) | async-done | bytes 9961504 | tf_op jit(solution)/shard_map/all_to_all | solution.py:28
  313.9 8.3 %fusion.24 = (f32[256]{0:T(256)S(1)}, f32[256,2432]{1,0:T(8,128)S(1)}) fusion(f32[256,2432]{1,0:T(8,128)} %convolution_bitcast_fusion, f32[256,2432]{1,0:T(8,128)} %convolution_bitcast_fusion.1, bf16[8,256,2432]{2,1,0:T(8,128)(2,1)} %all-to-all-done, bf16[256,8,256]{2,1,0:T(8,128)(2,1)S(1)} %get-tuple-element.30), kind=kOutput, calls=%fused_computation.63 | convolution fusion | flops 2552004352 | bytes 18482176 | tf_op jit(solution)/shard_map/dot_general | solution.py:40
  322.3 0.9 fusion.4
  323.2 0.5 copy-done.2
  323.7 0.7 broadcast_in_dim.4
  324.4 9.6 %all-to-all-start.3 = ((f32[32,4,256]{2,1,0:T(4,128)}), f32[32,4,256]{2,1,0:T(4,128)S(1)}, u32[]{:S(2)}, u32[]{:S(2)}) async-start(f32[32,4,256]{2,1,0:T(4,128)} %broadcast_in_dim.4), calls=%async_computation.3 | async-start | bytes 262144 | tf_op jit(solution)/shard_map/all_to_all | solution.py:14
  334.0 10.5 %all-to-all-done.3 = f32[32,4,256]{2,1,0:T(4,128)S(1)} async-done(((f32[32,4,256]{2,1,0:T(4,128)}), f32[32,4,256]{2,1,0:T(4,128)S(1)}, u32[]{:S(2)}, u32[]{:S(2)}) %all-to-all-start.3) | async-done | bytes 131104 | tf_op jit(solution)/shard_map/all_to_all | solution.py:14
  344.5 0.1 slice_reduce_fusion.2
  344.7 0.1 fusion.21
  344.8 0.6 broadcast_in_dim.5
  345.4 4.7 all-to-all-start.4
  350.1 3.9 all-to-all-done.4
  354.0 0.6 slice_reduce_fusion
  354.6 0.1 copy.70
  354.7 0.1 multiply_reduce_fusion.1
  355.5 0.8 fusion.18
  357.6 2.5 multiply_convert_fusion
  360.1 4.4 convolution_bitcast_fusion.5
  364.6 1.3 copy.58
  365.9 0.0 reduce-scatter.5.cloned.1.call-start
  365.9 5.5 %convolution_bitcast_fusion.4 = f32[2048,256]{0,1:T(8,128)S(1)} fusion(bf16[256,2432]{1,0:T(8,128)(2,1)S(1)} %multiply_convert_fusion, bf16[2048,2432]{1,0:T(8,128)(2,1)} %bitcast.20), kind=kOutput, calls=%fused_computation.6 | convolution fusion | flops 2550136832 | bytes 13303808 | tf_op jit(solution)/shard_map/dot_general | solution.py:93
  371.5 1.8 copy.56
  373.3 0.0 reduce-scatter.7.cloned.1.call-start
  373.4 5.5 %convolution_bitcast_fusion.3 = f32[2048,256]{0,1:T(8,128)S(1)} fusion(bf16[256,2432]{1,0:T(8,128)(2,1)S(1)} %multiply_convert_fusion, bf16[2048,2432]{1,0:T(8,128)(2,1)} %bitcast.115), kind=kOutput, calls=%fused_computation.5 | convolution fusion | flops 2550136832 | bytes 13303808 | tf_op jit(solution)/shard_map/dot_general | solution.py:93
  379.0 1.9 copy.57
  380.9 0.0 reduce-scatter.11.cloned.1.call-start
  380.9 17.7 %reduce-scatter.9.cloned.1.call-done = f32[1,128,256]{2,1,0:T(8,128)} async-done(((f32[8,128,256]{2,1,0:T(8,128)}), f32[1,128,256]{2,1,0:T(8,128)}) %reduce-scatter.9.cloned.1.call-update) | async-done | bytes 131088 | tf_op jit(solution)/shard_map/reduce_scatter | solution.py:96
  398.6 43.5 %reduce-scatter.5.cloned.1.call-done = f32[1,256,256]{2,1,0:T(8,128)} async-done(((f32[8,256,256]{2,1,0:T(8,128)}), f32[1,256,256]{2,1,0:T(8,128)}) %reduce-scatter.5.cloned.1.call-update) | async-done | bytes 262160 | tf_op jit(solution)/shard_map/reduce_scatter | solution.py:96
  442.1 43.5 %reduce-scatter.7.cloned.1.call-done = f32[1,256,256]{2,1,0:T(8,128)} async-done(((f32[8,256,256]{2,1,0:T(8,128)}), f32[1,256,256]{2,1,0:T(8,128)}) %reduce-scatter.7.cloned.1.call-update) | async-done | bytes 262160 | tf_op jit(solution)/shard_map/reduce_scatter | solution.py:96
  485.6 2.0 pad_maximum_fusion
  487.6 23.7 %reduce-scatter.11.cloned.1.call-done = f32[1,160,256]{2,1,0:T(8,128)} async-done(((f32[4,160,256]{2,1,0:T(8,128)}), f32[1,160,256]{2,1,0:T(8,128)}) %reduce-scatter.11.cloned.1.call-update) | async-done | bytes 163856 | tf_op jit(solution)/shard_map/reduce_scatter | solution.py:99
  511.3 1.6 copy_bitcast_fusion
  (33 shorter events, 0.3 us)
Async XLA Ops:
  10.9 63.5 %all-to-all-start.2 = ((bf16[8,128,2432]{2,1,0:T(8,128)(2,1)}), bf16[8,128,2432]{2,1,0:T(8,128)(2,1)}, u32[]{:S(2)}, u32[]{:S(2)}) async-start(bf16[8,128,2432]{2,1,0:T(8,128)(2,1)} %stack.25), calls=%async_computation.2 | async-start | bytes 9961472 | tf_op jit(solution)/shard_map/all_to_all | solution.py:28
  197.4 116.6 %all-to-all-start = ((bf16[8,256,2432]{2,1,0:T(8,128)(2,1)}), bf16[8,256,2432]{2,1,0:T(8,128)(2,1)}, u32[]{:S(2)}, u32[]{:S(2)}) async-start(bf16[8,256,2432]{2,1,0:T(8,128)(2,1)} %stack.23), calls=%async_computation | async-start | bytes 19922944 | tf_op jit(solution)/shard_map/all_to_all | solution.py:28
  203.8 3.9 copy-start
  206.1 1.5 copy-start.1
  322.2 1.5 copy-start.2
  322.2 22.5 %copy-start.6 = (s32[2,128]{1,0:T(2,128)S(1)}, s32[2,128]{1,0:T(2,128)}, u32[]{:S(2)}) copy-start(s32[2,128]{1,0:T(2,128)} %param.12) | copy-start | bytes 3076
  322.2 22.5 %copy-start.7 = (f32[2]{0:T(128)S(1)}, f32[2]{0:T(128)}, u32[]{:S(2)}) copy-start(f32[2]{0:T(128)} %param.13) | copy-start | bytes 28
  322.2 22.5 %copy-start.8 = (s32[2]{0:T(128)S(1)}, s32[2]{0:T(128)}, u32[]{:S(2)}) copy-start(s32[2]{0:T(128)} %param.11) | copy-start | bytes 28
  322.2 35.4 %copy-start.5 = (s32[2,128]{1,0:T(2,128)S(1)}, s32[2,128]{1,0:T(2,128)}, u32[]{:S(2)}) copy-start(s32[2,128]{1,0:T(2,128)} %param.10) | copy-start | bytes 3076
  324.4 20.1 %all-to-all-start.3 = ((f32[32,4,256]{2,1,0:T(4,128)}), f32[32,4,256]{2,1,0:T(4,128)S(1)}, u32[]{:S(2)}, u32[]{:S(2)}) async-start(f32[32,4,256]{2,1,0:T(4,128)} %broadcast_in_dim.4), calls=%async_computation.3 | async-start | bytes 262144 | tf_op jit(solution)/shard_map/all_to_all | solution.py:14
  345.4 8.6 %all-to-all-start.4 = ((f32[8,2,2,128]{3,2,1,0:T(2,128)}), f32[8,2,2,128]{3,2,1,0:T(2,128)S(1)}, u32[]{:S(2)}, u32[]{:S(2)}) async-start(f32[8,2,2,128]{3,2,1,0:T(2,128)} %broadcast_in_dim.5), calls=%async_computation.4 | async-start | bytes 32768 | tf_op jit(solution)/shard_map/all_to_all | solution.py:14
  350.1 48.5 %reduce-scatter.9.cloned.1.call-start = ((), (), s32[]{:S(2)}) async-start(), calls=%async_computation.11 | async-start | bytes 1179648 | tf_op jit(solution)/shard_map/reduce_scatter | solution.py:96
  357.6 6.9 %copy-start.4 = (f32[1,2,128]{2,0,1:T(1,128)}, f32[1,2,128]{2,0,1:T(1,128)S(1)}, u32[]{:S(2)}) copy-start(f32[1,2,128]{2,0,1:T(1,128)S(1)} %subtract_divide_fusion) | copy-start | bytes 3076
  360.1 13.3 %copy-start.3 = (bf16[256,2432]{1,0:T(8,128)(2,1)}, bf16[256,2432]{1,0:T(8,128)(2,1)S(1)}, u32[]{:S(2)}) copy-start(bf16[256,2432]{1,0:T(8,128)(2,1)S(1)} %multiply_convert_fusion) | copy-start | bytes 3735556
  365.9 76.2 %reduce-scatter.5.cloned.1.call-start = ((), (), s32[]{:S(2)}) async-start(), calls=%async_computation.9 | async-start | bytes 2359296 | tf_op jit(solution)/shard_map/reduce_scatter | solution.py:96
  373.3 112.2 %reduce-scatter.7.cloned.1.call-start = ((), (), s32[]{:S(2)}) async-start(), calls=%async_computation.10 | async-start | bytes 2359296 | tf_op jit(solution)/shard_map/reduce_scatter | solution.py:96
  380.9 130.5 %reduce-scatter.11.cloned.1.call-start = ((), (), s32[]{:S(2)}) async-start(), calls=%async_computation.12 | async-start | bytes 819200 | tf_op jit(solution)/shard_map/reduce_scatter | solution.py:99
Sparse Core Ops, SparseCore 0:
  366.0 32.5 reduce-scatter.8
  401.2 40.8 reduce-scatter.4
  444.7 40.8 reduce-scatter.6
  488.0 23.2 reduce-scatter.10
